TPU v7x, 32 devices: a whole 2x2x4 slice. The times are simulated.
32 devices in a mesh: seq: 16 (over z, y, core), head: 2 (over x).
Axes of the slice: x: 2, y: 2, z: 4, core: 2. Of those that a mesh axis runs over, the one named last changes fastest.
Arguments:
- queries: bfloat16 [8192, 4096], P(('seq', 'head')), may hold values from -64 to 64
- keys: bfloat16 [8192, 1024], P(('seq', 'head')), may hold values from -6 to 6
- values: bfloat16 [8192, 1024], P(('seq', 'head')), may hold values from -6 to 6
- level_bias: float32 [32, 4], P('head'), may hold values from -1 to 2
- anchor_bias: float32 [32], P('head'), may hold values from 1 to 4
- partners: int32 [16, 4], P('seq'), may hold values from 0 to 15, as said below
- anchor_positions: int32 [64], replicated, may hold values from 0 to 8191, as said below
Outputs:
- attended: bfloat16 [8192, 4096], P(('seq', 'head'))
Inputs may be any that keep to these rules, and one draw needn't show every extreme that they name: `partners`: row b holds b XOR 2**j once for each j of 0 to 3, in an order drawn for each block. `anchor_positions`: distinct positions.
All inputs are finite; a program needn't handle non-finite values.
Results may differ from a plain program's by a relative error of at most 0.0045.
Values may be sent and summed in bfloat16 or wider, within the bound.
A program may use at most 192 MiB of HBM per device.

v0:
```python
import functools

import jax
import jax.numpy as jnp
from jax import lax
from jax.experimental import pallas as pl
from jax.experimental.pallas import tpu as pltpu
from jax.sharding import PartitionSpec as P

HD = 128
LOG2E = 1.4426950408889634


def attend(query, key_parts, value_parts, biases, scale):
    scores = [
        lax.dot_general(query, k, (((1,), (1,)), ((), ())), preferred_element_type=jnp.float32)
        for k in key_parts
    ]
    row_max = None
    for s, b in zip(scores, biases):
        top = jnp.max(s, axis=1, keepdims=True) * scale + b
        row_max = top if row_max is None else jnp.maximum(row_max, top)
    total = None
    acc = None
    for s, v, b in zip(scores, value_parts, biases):
        p = jnp.exp2(s * scale + (b - row_max))
        part = jnp.sum(p, axis=1, keepdims=True)
        out = jnp.dot(p.astype(jnp.bfloat16), v, preferred_element_type=jnp.float32)
        total = part if total is None else total + part
        acc = out if acc is None else acc + out
    return acc / total


def kernel(
    heads, levels, kv_local, group,
    level_ref, anchor_ref, partners_ref, places_ref, keys_ref, values_ref, queries_ref, out_ref,
    blocks, qbuf, obuf, part, part_in, carry, carry_in,
    part_send, part_recv, carry_send, carry_recv,
    own_sem, x_send, x_recv, own_q_sem, q_send, q_recv,
    lv_send, lv_recv, own_o_sem, o_send, o_recv,
):
    me = lax.axis_index("head")
    seat = lax.axis_index("seq")
    t = keys_ref.shape[0]
    wide = group * HD
    scale = HD ** -0.5 * LOG2E
    mesh_id = pl.DeviceIdType.MESH

    def peer(d):
        return lax.rem(me + d, heads)

    def partner(l):
        bit = lax.rem(lax.div(seat, 1 << l), 2)
        return seat + (1 - 2 * bit) * (1 << l)

    barrier = pltpu.get_barrier_semaphore()
    for d in range(1, heads):
        pl.semaphore_signal(barrier, inc=1, device_id={"head": peer(d)}, device_id_type=mesh_id)
    for l in range(levels):
        pl.semaphore_signal(barrier, inc=1, device_id={"seq": partner(l)}, device_id_type=mesh_id)

    def cols(owner, j, width):
        return pl.ds(pl.multiple_of((owner * kv_local + j) * width, width), width)

    def rows(owner):
        return pl.ds(pl.multiple_of(owner * t, t), t)

    def own_copy(j, c):
        src = (keys_ref, values_ref)[c]
        return pltpu.make_async_copy(
            src.at[:, cols(me, j, HD)], blocks.at[0, j, c, rows(me)], own_sem.at[j, c])

    def own_q(j):
        return pltpu.make_async_copy(
            queries_ref.at[:, cols(me, j, wide)], qbuf.at[j, rows(me)], own_q_sem.at[j])

    def send_kv(j, c, d):
        src = (keys_ref, values_ref)[c]
        return pltpu.make_async_remote_copy(
            src_ref=src.at[:, cols(peer(d), j, HD)], dst_ref=blocks.at[0, j, c, rows(me)],
            send_sem=x_send.at[j, c, d], recv_sem=x_recv.at[j, c, d],
            device_id={"head": peer(d)}, device_id_type=mesh_id)

    def came_kv(j, c, d):
        src = (keys_ref, values_ref)[c]
        return pltpu.make_async_remote_copy(
            src_ref=src.at[:, cols(me, j, HD)], dst_ref=blocks.at[0, j, c, rows(peer(heads - d))],
            send_sem=x_send.at[j, c, d], recv_sem=x_recv.at[j, c, d],
            device_id={"head": peer(d)}, device_id_type=mesh_id)

    def send_q(j, d):
        return pltpu.make_async_remote_copy(
            src_ref=queries_ref.at[:, cols(peer(d), j, wide)], dst_ref=qbuf.at[j, rows(me)],
            send_sem=q_send.at[j, d], recv_sem=q_recv.at[j, d],
            device_id={"head": peer(d)}, device_id_type=mesh_id)

    def came_q(j, d):
        return pltpu.make_async_remote_copy(
            src_ref=queries_ref.at[:, cols(me, j, wide)], dst_ref=qbuf.at[j, rows(peer(heads - d))],
            send_sem=q_send.at[j, d], recv_sem=q_recv.at[j, d],
            device_id={"head": peer(d)}, device_id_type=mesh_id)

    def send_level(j, l):
        return pltpu.make_async_remote_copy(
            src_ref=blocks.at[0, j], dst_ref=blocks.at[l + 1, j],
            send_sem=lv_send.at[j, l], recv_sem=lv_recv.at[j, l],
            device_id={"seq": partner(l)}, device_id_type=mesh_id)

    def send_part(d):
        return pltpu.make_async_remote_copy(
            src_ref=part.at[d], dst_ref=part_in.at[d],
            send_sem=part_send.at[d], recv_sem=part_recv.at[d],
            device_id={"head": peer(d)}, device_id_type=mesh_id)

    def send_carry(l):
        return pltpu.make_async_remote_copy(
            src_ref=carry.at[l + 1], dst_ref=carry_in.at[l],
            send_sem=carry_send.at[l], recv_sem=carry_recv.at[l],
            device_id={"seq": partner(l)}, device_id_type=mesh_id)

    def send_out(j, d):
        return pltpu.make_async_remote_copy(
            src_ref=obuf.at[j, d], dst_ref=out_ref.at[:, cols(me, j, wide)],
            send_sem=o_send.at[j, d], recv_sem=o_recv.at[j, d],
            device_id={"head": peer(d)}, device_id_type=mesh_id)

    def came_out(j, d):
        return pltpu.make_async_remote_copy(
            src_ref=obuf.at[j, d], dst_ref=out_ref.at[:, cols(peer(heads - d), j, wide)],
            send_sem=o_send.at[j, d], recv_sem=o_recv.at[j, d],
            device_id={"head": peer(d)}, device_id_type=mesh_id)

    def own_out(j):
        return pltpu.make_async_copy(
            obuf.at[j, 0], out_ref.at[:, cols(me, j, wide)], own_o_sem.at[j])

    for j in range(kv_local):
        for c in range(2):
            own_copy(j, c).start()
        own_q(j).start()
    first = (seat * heads + me) * t
    places = places_ref[...] - first
    token = lax.broadcasted_iota(jnp.int32, (places.shape[0], t), 1)
    selector = jnp.where(places == token, 1.0, 0.0).astype(jnp.bfloat16)
    for d in range(heads):
        for j in range(kv_local):
            for c in range(2):
                src = (keys_ref, values_ref)[c]
                part[d, j, c] = jnp.dot(
                    selector, src[:, cols(peer(d), j, HD)], preferred_element_type=jnp.float32
                ).astype(jnp.bfloat16)
    pl.semaphore_wait(barrier, heads - 1 + levels)
    for d in range(1, heads):
        send_part(d).start()
    for j in range(kv_local):
        for d in range(1, heads):
            for c in range(2):
                send_kv(j, c, d).start()
    for j in range(kv_local):
        for d in range(1, heads):
            send_q(j, d).start()

    def forward(j):
        for c in range(2):
            own_copy(j, c).wait()
            for d in range(1, heads):
                came_kv(j, c, d).wait_recv()
        for l in reversed(range(levels)):
            send_level(j, l).start()

    held = part[0].astype(jnp.float32)
    for d in range(1, heads):
        send_part(d).wait_recv()
        held = held + part_in[d].astype(jnp.float32)
    carry[levels] = held.astype(jnp.bfloat16)
    for l in reversed(range(levels)):
        send_carry(l).start()
        if levels - 1 - l < kv_local:
            forward(levels - 1 - l)
        send_carry(l).wait_recv()
        carry[l] = (carry[l + 1].astype(jnp.float32) + carry_in[l].astype(jnp.float32)).astype(
            jnp.bfloat16)
    for j in range(levels, kv_local):
        forward(j)

    def biases(h):
        found = [jnp.float32(0.0)]
        for l in range(levels):
            total = jnp.float32(0.0)
            for m in range(levels):
                total += jnp.where(partners_ref[0, m] == partner(l), level_ref[h, m], 0.0)
            found.append(total * LOG2E)
        return found + [anchor_ref[h] * LOG2E]

    def one(step, _):
        j = lax.div(step, heads)
        turn = lax.rem(step, heads)

        @pl.when(turn == 0)
        def _():
            own_q(j).wait()
            for d in range(1, heads):
                came_q(j, d).wait_recv()
            for l in range(levels):
                send_level(j, l).wait_recv()

        d = lax.rem(turn + 1, heads)
        here = rows(peer(d))
        for g in range(group):
            result = attend(
                qbuf[j, here, g * HD:(g + 1) * HD],
                [blocks[n, j, 0] for n in range(levels + 1)] + [carry[0, j, 0]],
                [blocks[n, j, 1] for n in range(levels + 1)] + [carry[0, j, 1]],
                biases(j * group + g),
                scale,
            )
            obuf[j, d, :, g * HD:(g + 1) * HD] = result.astype(jnp.bfloat16)

        @pl.when(turn < heads - 1)
        def _():
            send_out(j, d).start()

        @pl.when(turn == heads - 1)
        def _():
            own_out(j).start()

        return 0

    lax.fori_loop(0, kv_local * heads, one, 0)

    for d in range(1, heads):
        send_part(d).wait_send()
    for l in range(levels):
        send_carry(l).wait_send()
    for j in range(kv_local):
        own_out(j).wait()
        for l in range(levels):
            send_level(j, l).wait_send()
        for d in range(1, heads):
            for c in range(2):
                send_kv(j, c, d).wait_send()
            send_q(j, d).wait_send()
            send_out(j, d).wait_send()
            came_out(j, d).wait_recv()


def on_device(queries, keys, values, level_bias, anchor_bias, partners, anchor_positions):
    t = queries.shape[0]
    heads = lax.axis_size("head")
    levels = lax.axis_size("seq").bit_length() - 1
    kv_local = keys.shape[1] // HD // heads
    group = level_bias.shape[0] // kv_local
    anchors = anchor_positions.shape[0]
    smem = pl.BlockSpec(memory_space=pltpu.SMEM)
    vmem = pl.BlockSpec(memory_space=pltpu.VMEM)
    dma = pltpu.SemaphoreType.DMA
    anchor_shape = (kv_local, 2, anchors, HD)
    bf16 = jnp.bfloat16
    return pl.pallas_call(
        functools.partial(kernel, heads, levels, kv_local, group),
        in_specs=[smem, smem, smem, vmem, vmem, vmem,
                  pl.BlockSpec(memory_space=pl.ANY)],
        out_specs=pl.BlockSpec(memory_space=pl.ANY),
        out_shape=jax.ShapeDtypeStruct(queries.shape, queries.dtype),
        scratch_shapes=[
            pltpu.VMEM((levels + 1, kv_local, 2, t * heads, HD), bf16),
            pltpu.VMEM((kv_local, t * heads, group * HD), bf16),
            pltpu.VMEM((kv_local, heads, t, group * HD), bf16),
            pltpu.VMEM((heads,) + anchor_shape, bf16),
            pltpu.VMEM((heads,) + anchor_shape, bf16),
            pltpu.VMEM((levels + 1,) + anchor_shape, bf16),
            pltpu.VMEM((levels,) + anchor_shape, bf16),
            dma((heads,)), dma((heads,)), dma((levels,)), dma((levels,)),
            dma((kv_local, 2)), dma((kv_local, 2, heads)), dma((kv_local, 2, heads)),
            dma((kv_local,)), dma((kv_local, heads)), dma((kv_local, heads)),
            dma((kv_local, levels)), dma((kv_local, levels)),
            dma((kv_local,)), dma((kv_local, heads)), dma((kv_local, heads)),
        ],
        compiler_params=pltpu.CompilerParams(collective_id=0, has_side_effects=True),
        name="attend",
    )(level_bias, anchor_bias, partners, anchor_positions[:, None], keys, values, queries)


def solution(mesh):
    in_specs = (
        P(("seq", "head"), None),
        P(("seq", "head"), None),
        P(("seq", "head"), None),
        P("head", None),
        P("head"),
        P("seq", None),
        P(),
    )
    out_specs = P(("seq", "head"), None)
    return jax.shard_map(
        on_device, mesh=mesh, in_specs=in_specs, out_specs=out_specs, check_vma=False
    )
```

profile of v0, /device:TPU:0, one launch (start us, length us, event | category | flops | bytes accessed | tf_op | source)
XLA Modules:
  0.0 84.2 jit_solution(16161751010593163050)
XLA Ops:
  0.0 1.4 %copy.8.level_ref = f32[16,4]{1,0:T(8,128)} copy(f32[16,4]{0,1:T(4,128)} %param.10) | data formatting | bytes 512 | tf_op args[3]
  1.4 1.4 %copy.9.places_ref = s32[64,1]{1,0:T(8,128)} copy(s32[64,1]{0,1:T(1,128)} %bitcast.1) | data formatting | bytes 512 | tf_op jit(solution)/shard_map/broadcast_in_dim | solution.py:281
  2.7 78.4 %attend.1 = bf16[256,4096]{1,0:T(8,128)(2,1)} custom-call(f32[16,4]{1,0:T(8,128)} %copy.8.level_ref, f32[16]{0:T(128)} %anchor_ref.1, s32[1,4]{1,0:T(1,128)} %partners_ref.1, s32[64,1]{1,0:T(8,128)} %copy.9.places_ref, bf16[256,1024]{1,0:T(8,128)(2,1)} %keys_ref.1, bf16[256,1024]{1,0:T(8,128)(2,1)} %values_ref.1, bf16[256,4096]{1,0:T(8,128)(2,1)} %queries_ref.1), custom_call_target="tpu_custom_call" | custom-call | tf_op jit(solution)/shard_map/attend/pallas_call | solution.py:259
  81.1 3.1 %copy.11 = bf16[256,4096]{1,0:T(8,128)(2,1)} copy(bf16[256,4096]{1,0:T(8,128)(2,1)} %attend.1) | data formatting | bytes 4194304
where the time goes:
time: 84.4 us; the launch traced here: 84.2 us
  Pallas kernels  78.4 us (93%)
  local copies, waits for them, and re-layouts  5.84 us (7%)
    pallas_call x1, Pallas kernels, on_device(): pl.pallas_call(functools.partial(kernel, heads, levels, kv_local, group),...  78.4 us
    unnamed x2, local copies, waits for them, and re-layouts  4.48 us

commit v1 on v0

v1 whole, which is shorter than its diff:
```python
import functools

import jax
import jax.numpy as jnp
from jax import lax
from jax.experimental import pallas as pl
from jax.experimental.pallas import tpu as pltpu
from jax.sharding import PartitionSpec as P

HD = 128
LOG2E = 1.4426950408889634


def attend(query, key_parts, value_parts, biases, scale):
    scores = [
        lax.dot_general(query, k, (((1,), (1,)), ((), ())), preferred_element_type=jnp.float32)
        for k in key_parts
    ]
    row_max = None
    for s, b in zip(scores, biases):
        top = jnp.max(s, axis=1, keepdims=True) * scale + b
        row_max = top if row_max is None else jnp.maximum(row_max, top)
    total = None
    acc = None
    for s, v, b in zip(scores, value_parts, biases):
        p = jnp.exp2(s * scale + (b - row_max))
        part = jnp.sum(p, axis=1, keepdims=True)
        out = jnp.dot(p.astype(jnp.bfloat16), v, preferred_element_type=jnp.float32)
        total = part if total is None else total + part
        acc = out if acc is None else acc + out
    return acc / total


def kernel(
    heads, levels, kv_local, group,
    level_ref, anchor_ref, partners_ref, places_ref, keys_ref, values_ref, queries_ref, out_ref,
    kv, qbuf, obuf, full, part, part_in, head_out, head_in, carry, carry_in, table,
    own_sem, full_sem, own_q_sem, own_o_sem,
    x_send, x_recv, q_send, q_recv, o_send, o_recv, lv_send, lv_recv,
    core_send, core_recv, head_send, head_recv, carry_send, carry_recv,
    last_sem, last_send, last_recv,
):
    me = lax.axis_index("head")
    seat = lax.axis_index("seq")
    t = keys_ref.shape[0]
    block = heads * t
    wide = group * HD
    anchors = places_ref.shape[1]
    scale = HD ** -0.5 * LOG2E
    mesh_id = pl.DeviceIdType.MESH
    bf16 = jnp.bfloat16
    sources = (keys_ref, values_ref)
    mine = lax.rem(seat, 2)

    def peer(d):
        return lax.rem(me + d, heads)

    def partner(l):
        bit = lax.rem(lax.div(seat, 1 << l), 2)
        return seat + (1 - 2 * bit) * (1 << l)

    def cols(owner, j, width):
        return pl.ds(pl.multiple_of((owner * kv_local + j) * width, width), width)

    def rows(n, r):
        return pl.ds(pl.multiple_of(n * block + r * t, t), t)

    anchor_rows = pl.ds((levels + 1) * block, anchors)

    def to_head(src, dst, send, recv, d):
        return pltpu.make_async_remote_copy(
            src_ref=src, dst_ref=dst, send_sem=send, recv_sem=recv,
            device_id={"head": peer(d)}, device_id_type=mesh_id)

    def to_level(src, dst, send, recv, l):
        return pltpu.make_async_remote_copy(
            src_ref=src, dst_ref=dst, send_sem=send, recv_sem=recv,
            device_id={"seq": partner(l)}, device_id_type=mesh_id)

    def own_copy(j, c):
        return pltpu.make_async_copy(
            sources[c].at[:, cols(me, j, HD)], kv.at[j, c, rows(0, me)], own_sem.at[j, c])

    def full_copy(c):
        return pltpu.make_async_copy(sources[c], full.at[c], full_sem.at[c])

    def own_q(j):
        return pltpu.make_async_copy(
            queries_ref.at[:, cols(me, j, wide)], qbuf.at[j, 0], own_q_sem.at[j])

    def send_kv(j, c, d):
        return to_head(
            sources[c].at[:, cols(peer(d), j, HD)], kv.at[j, c, rows(0, me)],
            x_send.at[j, c, d], x_recv.at[j, c, d], d)

    def came_kv(j, c, d):
        return to_head(
            sources[c].at[:, cols(me, j, HD)], kv.at[j, c, rows(0, peer(heads - d))],
            x_send.at[j, c, d], x_recv.at[j, c, d], d)

    def send_q(j, d):
        return to_head(
            queries_ref.at[:, cols(peer(d), j, wide)], qbuf.at[j, d],
            q_send.at[j, d], q_recv.at[j, d], d)

    def send_level(j, c, d, l):
        r = peer(heads - d)
        src = sources[c].at[:, cols(me, j, HD)] if d == 0 else kv.at[j, c, rows(0, r)]
        return to_level(
            src, kv.at[j, c, rows(l + 1, r)],
            lv_send.at[j, c, d, l], lv_recv.at[j, c, d, l], l)

    def level_came(j, c, d, l):
        r = peer(heads - d)
        return to_level(
            kv.at[j, c, rows(0, r)], kv.at[j, c, rows(l + 1, r)],
            lv_send.at[j, c, d, l], lv_recv.at[j, c, d, l], l)

    def send_core():
        return to_level(part.at[1 - mine], part_in, core_send, core_recv, 0)

    def send_part(d):
        return to_head(head_out.at[d], head_in.at[d], head_send.at[d], head_recv.at[d], d)

    def send_carry(i, l):
        return to_level(carry.at[i], carry_in.at[i], carry_send.at[i], carry_recv.at[i], l)

    def own_last(j):
        return pltpu.make_async_copy(
            carry.at[levels - 1, j], kv.at[j, mine, anchor_rows], last_sem.at[j])

    def send_last(j):
        return to_level(
            carry.at[levels - 1, j], kv.at[j, mine, anchor_rows],
            last_send.at[j], last_recv.at[j], 0)

    def last_came(j):
        return to_level(
            carry.at[levels - 1, j], kv.at[j, 1 - mine, anchor_rows],
            last_send.at[j], last_recv.at[j], 0)

    def out_cols(owner, j, g):
        return pl.ds(pl.multiple_of(((owner * kv_local + j) * group + g) * HD, HD), HD)

    def send_out(j, g, d):
        return to_head(
            obuf.at[j, d, g], out_ref.at[:, out_cols(me, j, g)],
            o_send.at[j, g, d], o_recv.at[j, g, d], heads - d)

    def came_out(j, g, d):
        return to_head(
            obuf.at[j, d, g], out_ref.at[:, out_cols(peer(d), j, g)],
            o_send.at[j, g, d], o_recv.at[j, g, d], heads - d)

    def own_out(j, g):
        return pltpu.make_async_copy(
            obuf.at[j, 0, g], out_ref.at[:, out_cols(me, j, g)], own_o_sem.at[j, g])

    barrier = pltpu.get_barrier_semaphore()
    for d in range(1, heads):
        pl.semaphore_signal(barrier, inc=1, device_id={"head": peer(d)}, device_id_type=mesh_id)
    for l in range(levels):
        pl.semaphore_signal(barrier, inc=1, device_id={"seq": partner(l)}, device_id_type=mesh_id)

    for c in range(2):
        full_copy(c).start()
    for j in range(kv_local):
        for c in range(2):
            own_copy(j, c).start()
    pl.semaphore_wait(barrier, heads - 1 + levels)

    far = list(reversed(range(levels)))

    def push_kv(j):
        for d in range(1, heads):
            for c in range(2):
                send_kv(j, c, d).start()

    def push_levels(j, c, d):
        for l in far:
            send_level(j, c, d, l).start()

    push_kv(0)
    for c in range(2):
        push_levels(0, c, 0)

    first = (seat * heads + me) * t
    places = places_ref[...] - first
    token = lax.broadcasted_iota(jnp.int32, (t, anchors), 0)
    selector = jnp.where(places == token, 1.0, 0.0).astype(bf16)
    for c in range(2):
        full_copy(c).wait()
        for d in range(heads):
            for j in range(kv_local):
                part[c, d, j] = lax.dot_general(
                    selector, full[c, :, cols(peer(d), j, HD)], (((0,), (0,)), ((), ())),
                    preferred_element_type=jnp.float32).astype(bf16)
    send_core().start()
    send_core().wait_recv()
    for d in range(heads):
        head_out[d] = (
            part[mine, d].astype(jnp.float32) + part_in[d].astype(jnp.float32)).astype(bf16)
    for d in range(1, heads):
        send_part(d).start()
    for j in range(1, kv_local):
        push_kv(j)
    for j in range(kv_local):
        for d in range(1, heads):
            send_q(j, d).start()
        own_q(j).start()

    def wait_kv(j, c):
        own_copy(j, c).wait()
        for d in range(1, heads):
            came_kv(j, c, d).wait_recv()

    pending = [(0, c, d) for c in range(2) for d in range(1, heads)]
    for j in range(1, kv_local):
        pending += [(j, c, 0) for c in range(2)]
        pending += [(j, c, d) for c in range(2) for d in range(1, heads)]

    def push(count):
        for _ in range(min(count, len(pending))):
            j, c, d = pending.pop(0)
            if d == 0:
                own_copy(j, c).wait()
            else:
                came_kv(j, c, d).wait_recv()
            push_levels(j, c, d)

    for c in range(2):
        own_copy(0, c).wait()

    def fill(h, _):
        for l in range(levels):
            total = jnp.float32(0.0)
            for m in range(levels):
                total += jnp.where(partners_ref[0, m] == partner(l), level_ref[m, h], 0.0)
            table[l, h] = total * LOG2E
        table[levels, h] = anchor_ref[h] * LOG2E
        return 0

    lax.fori_loop(0, kv_local * group, fill, 0)

    held = head_out[0].astype(jnp.float32)
    for d in range(1, heads):
        send_part(d).wait_recv()
        held = held + head_in[d].astype(jnp.float32)
    carry[0] = held.astype(bf16)
    order = list(range(2, levels)) + ([1] if levels > 1 else [])
    for i, l in enumerate(order):
        send_carry(i, l).start()
        push(1)
        send_carry(i, l).wait_recv()
        carry[i + 1] = (
            carry[i].astype(jnp.float32) + carry_in[i].astype(jnp.float32)).astype(bf16)
    for j in range(kv_local):
        own_last(j).start()
        send_last(j).start()
    push(len(pending))

    def one(step, _):
        j = lax.div(step, heads)
        turn = lax.rem(step, heads)

        @pl.when(turn == 0)
        def _():
            own_last(j).wait()
            last_came(j).wait_recv()
            for l in range(levels):
                for c in range(2):
                    for d in range(heads):
                        level_came(j, c, d, l).wait_recv()

        d = lax.rem(turn + 1, heads)

        @pl.when(turn < heads - 1)
        def _():
            send_q(j, d).wait_recv()

        @pl.when(turn == heads - 1)
        def _():
            own_q(j).wait()

        for g in range(group):
            h = j * group + g
            result = attend(
                qbuf[j, d, :, g * HD:(g + 1) * HD],
                [kv[j, 0, n * block:(n + 1) * block] for n in range(levels + 1)]
                + [kv[j, 0, (levels + 1) * block:]],
                [kv[j, 1, n * block:(n + 1) * block] for n in range(levels + 1)]
                + [kv[j, 1, (levels + 1) * block:]],
                [jnp.float32(0.0)] + [table[l, h] for l in range(levels + 1)],
                scale,
            )
            obuf[j, d, g] = result.astype(bf16)

            @pl.when(turn < heads - 1)
            def _():
                send_out(j, g, d).start()

            @pl.when(turn == heads - 1)
            def _():
                own_out(j, g).start()

        return 0

    lax.fori_loop(0, kv_local * heads, one, 0)

    send_core().wait_send()
    for d in range(1, heads):
        send_part(d).wait_send()
    for i, l in enumerate(order):
        send_carry(i, l).wait_send()
    for j in range(kv_local):
        send_last(j).wait_send()
        for c in range(2):
            for d in range(heads):
                for l in range(levels):
                    send_level(j, c, d, l).wait_send()
            for d in range(1, heads):
                send_kv(j, c, d).wait_send()
        for d in range(1, heads):
            send_q(j, d).wait_send()
        for g in range(group):
            own_out(j, g).wait()
            for d in range(1, heads):
                send_out(j, g, d).wait_send()
                came_out(j, g, d).wait_recv()


def on_device(queries, keys, values, level_bias, anchor_bias, partners, anchor_positions):
    t = queries.shape[0]
    heads = lax.axis_size("head")
    levels = lax.axis_size("seq").bit_length() - 1
    kv_local = keys.shape[1] // HD // heads
    group = level_bias.shape[0] // kv_local
    anchors = anchor_positions.shape[0]
    smem = pl.BlockSpec(memory_space=pltpu.SMEM)
    vmem = pl.BlockSpec(memory_space=pltpu.VMEM)
    hbm = pl.BlockSpec(memory_space=pl.ANY)
    dma = pltpu.SemaphoreType.DMA
    anchor_shape = (kv_local, anchors, HD)
    bf16 = jnp.bfloat16
    return pl.pallas_call(
        functools.partial(kernel, heads, levels, kv_local, group),
        in_specs=[smem, smem, smem, vmem, hbm, hbm, hbm],
        out_specs=hbm,
        out_shape=jax.ShapeDtypeStruct(queries.shape, queries.dtype),
        scratch_shapes=[
            pltpu.VMEM((kv_local, 2, (levels + 1) * heads * t + anchors, HD), bf16),
            pltpu.VMEM((kv_local, heads, t, group * HD), bf16),
            pltpu.VMEM((kv_local, heads, group, t, HD), bf16),
            pltpu.VMEM((2,) + keys.shape, bf16),
            pltpu.VMEM((2, heads) + anchor_shape, bf16),
            pltpu.VMEM((heads,) + anchor_shape, bf16),
            pltpu.VMEM((heads,) + anchor_shape, bf16),
            pltpu.VMEM((heads,) + anchor_shape, bf16),
            pltpu.VMEM((levels,) + anchor_shape, bf16),
            pltpu.VMEM((levels,) + anchor_shape, bf16),
            pltpu.SMEM((levels + 1, kv_local * group), jnp.float32),
            dma((kv_local, 2)), dma((2,)), dma((kv_local,)), dma((kv_local, group)),
            dma((kv_local, 2, heads)), dma((kv_local, 2, heads)),
            dma((kv_local, heads)), dma((kv_local, heads)),
            dma((kv_local, group, heads)), dma((kv_local, group, heads)),
            dma((kv_local, 2, heads, levels)), dma((kv_local, 2, heads, levels)),
            dma, dma, dma((heads,)), dma((heads,)), dma((levels,)), dma((levels,)),
            dma((kv_local,)), dma((kv_local,)), dma((kv_local,)),
        ],
        compiler_params=pltpu.CompilerParams(collective_id=0, has_side_effects=True),
        name="attend",
    )(level_bias.T, anchor_bias, partners, anchor_positions[None, :], keys, values, queries)


def solution(mesh):
    in_specs = (
        P(("seq", "head"), None),
        P(("seq", "head"), None),
        P(("seq", "head"), None),
        P("head", None),
        P("head"),
        P("seq", None),
        P(),
    )
    out_specs = P(("seq", "head"), None)
    return jax.shard_map(
        on_device, mesh=mesh, in_specs=in_specs, out_specs=out_specs, check_vma=False
    )
```

time: 84.4 us -> 78.7 us (0.932)
  Pallas kernels: 78.4 us -> 75.4 us
  local copies, waits for them, and re-layouts: 5.84 us -> 3.13 us
    pallas_call x1, Pallas kernels: 78.4 us -> 75.4 us  [on_device(): pl.pallas_call(functools.partial(kernel, heads, levels, kv_local, group),...]
    broadcast_in_dim x1 -> x0, local copies, waits for them, and re-layouts: 1.36 us -> none  [on_device(): anchor_positions[:, None]]
    unnamed x2 -> x1, local copies, waits for them, and re-layouts: 4.48 us -> 3.13 us
where the time goes in v1:
time: 78.7 us; the launch traced here: 78.5 us
  Pallas kernels  75.4 us (96%)
  local copies, waits for them, and re-layouts  3.13 us (4%)
    pallas_call x1, Pallas kernels, on_device(): pl.pallas_call(functools.partial(kernel, heads, levels, kv_local, group),...  75.4 us
    unnamed x1, local copies, waits for them, and re-layouts  3.13 us

profile of v1, /device:TPU:0, one launch (start us, length us, event | category | flops | bytes accessed | tf_op | source)
XLA Modules:
  0.0 78.5 jit_solution(15853821547792172724)
XLA Ops:
  0.0 75.4 %attend.1 = bf16[256,4096]{1,0:T(8,128)(2,1)} custom-call(f32[4,16]{1,0:T(4,128)} %bitcast.2, f32[16]{0:T(128)} %anchor_ref.1, s32[1,4]{1,0:T(1,128)} %partners_ref.1, s32[1,64]{1,0:T(1,128)} %bitcast.3, bf16[256,1024]{1,0:T(8,128)(2,1)} %keys_ref.1, bf16[256,1024]{1,0:T(8,128)(2,1)} %values_ref.1, bf16[256,4096]{1,0:T(8,128)(2,1)} %queries_ref.1), custom_call_target="tpu_custom_call" | custom-call | tf_op jit(solution)/shard_map/attend/pallas_call | solution.py:345
  75.4 3.1 %copy.9 = bf16[256,4096]{1,0:T(8,128)(2,1)} copy(bf16[256,4096]{1,0:T(8,128)(2,1)} %attend.1) | data formatting | bytes 4194304

commit v2 on v1

--- a/solution.py
+++ b/solution.py
@@ -11,31 +11,35 @@
 LOG2E = 1.4426950408889634
 
 
-def attend(query, key_parts, value_parts, biases, scale):
+def attend(query, keys, values, biases, scale):
+    scaled = query.astype(jnp.float32) * scale
+    high = scaled.astype(jnp.bfloat16)
+    low = (scaled - high.astype(jnp.float32)).astype(jnp.bfloat16)
+    query = jnp.concatenate([high, low], axis=1)
     scores = [
-        lax.dot_general(query, k, (((1,), (1,)), ((), ())), preferred_element_type=jnp.float32)
-        for k in key_parts
+        lax.dot_general(
+            query, jnp.concatenate([k, k], axis=1), (((1,), (1,)), ((), ())),
+            preferred_element_type=jnp.float32)
+        for k in keys
     ]
     row_max = None
     for s, b in zip(scores, biases):
-        top = jnp.max(s, axis=1, keepdims=True) * scale + b
+        top = jnp.max(s, axis=1, keepdims=True) + b
         row_max = top if row_max is None else jnp.maximum(row_max, top)
-    total = None
-    acc = None
-    for s, v, b in zip(scores, value_parts, biases):
-        p = jnp.exp2(s * scale + (b - row_max))
-        part = jnp.sum(p, axis=1, keepdims=True)
-        out = jnp.dot(p.astype(jnp.bfloat16), v, preferred_element_type=jnp.float32)
-        total = part if total is None else total + part
-        acc = out if acc is None else acc + out
-    return acc / total
+    weights = jnp.concatenate(
+        [jnp.exp2(s - (row_max - b)).astype(jnp.bfloat16) for s, b in zip(scores, biases)], axis=1)
+    both = jnp.dot(
+        weights, jnp.concatenate([values, jnp.ones_like(values)], axis=1),
+        preferred_element_type=jnp.float32)
+    return both[:, :HD] / both[:, HD:]
 
 
 def kernel(
     heads, levels, kv_local, group,
-    level_ref, anchor_ref, partners_ref, places_ref, keys_ref, values_ref, queries_ref, out_ref,
+    level_hbm, anchor_hbm, partners_hbm, places_hbm, keys_ref, values_ref, queries_ref, out_ref,
+    level_ref, anchor_ref, partners_ref, places_ref, small_sem,
     kv, qbuf, obuf, full, part, part_in, head_out, head_in, carry, carry_in, table,
-    own_sem, full_sem, own_q_sem, own_o_sem,
+    own_sem, full_sem, own_q_sem,
     x_send, x_recv, q_send, q_recv, o_send, o_recv, lv_send, lv_recv,
     core_send, core_recv, head_send, head_recv, carry_send, carry_recv,
     last_sem, last_send, last_recv,
@@ -152,9 +156,10 @@
             obuf.at[j, d, g], out_ref.at[:, out_cols(peer(d), j, g)],
             o_send.at[j, g, d], o_recv.at[j, g, d], heads - d)
 
-    def own_out(j, g):
-        return pltpu.make_async_copy(
-            obuf.at[j, 0, g], out_ref.at[:, out_cols(me, j, g)], own_o_sem.at[j, g])
+    def small(i):
+        src = (level_hbm, anchor_hbm, partners_hbm, places_hbm)[i]
+        dst = (level_ref, anchor_ref, partners_ref, places_ref)[i]
+        return pltpu.make_async_copy(src, dst, small_sem.at[i])
 
     barrier = pltpu.get_barrier_semaphore()
     for d in range(1, heads):
@@ -164,9 +169,12 @@
 
     for c in range(2):
         full_copy(c).start()
+    for i in range(4):
+        small(i).start()
     for j in range(kv_local):
         for c in range(2):
             own_copy(j, c).start()
+        own_q(j).start()
     pl.semaphore_wait(barrier, heads - 1 + levels)
 
     far = list(reversed(range(levels)))
@@ -184,6 +192,7 @@
     for c in range(2):
         push_levels(0, c, 0)
 
+    small(3).wait()
     first = (seat * heads + me) * t
     places = places_ref[...] - first
     token = lax.broadcasted_iota(jnp.int32, (t, anchors), 0)
@@ -207,7 +216,6 @@
     for j in range(kv_local):
         for d in range(1, heads):
             send_q(j, d).start()
-        own_q(j).start()
 
     def wait_kv(j, c):
         own_copy(j, c).wait()
@@ -230,6 +238,9 @@
 
     for c in range(2):
         own_copy(0, c).wait()
+
+    for i in range(3):
+        small(i).wait()
 
     def fill(h, _):
         for l in range(levels):
@@ -259,53 +270,39 @@
         send_last(j).start()
     push(len(pending))
 
-    def one(step, _):
-        j = lax.div(step, heads)
-        turn = lax.rem(step, heads)
-
-        @pl.when(turn == 0)
-        def _():
-            own_last(j).wait()
-            last_came(j).wait_recv()
-            for l in range(levels):
-                for c in range(2):
-                    for d in range(heads):
-                        level_came(j, c, d, l).wait_recv()
-
-        d = lax.rem(turn + 1, heads)
-
-        @pl.when(turn < heads - 1)
-        def _():
+    def answer(j, d, g):
+        return attend(
+            qbuf[j, d, :, g * HD:(g + 1) * HD],
+            [kv[j, 0, n * block:(n + 1) * block] for n in range(levels + 1)]
+            + [kv[j, 0, (levels + 1) * block:]],
+            kv[j, 1],
+            [jnp.float32(0.0)] + [table[l, j * group + g] for l in range(levels + 1)],
+            scale,
+        ).astype(bf16)
+
+    def one(j, _):
+        own_last(j).wait()
+        last_came(j).wait_recv()
+        for l in range(levels):
+            for c in range(2):
+                for d in range(heads):
+                    level_came(j, c, d, l).wait_recv()
+
+        def remote(i, _):
+            d = i + 1
             send_q(j, d).wait_recv()
-
-        @pl.when(turn == heads - 1)
-        def _():
-            own_q(j).wait()
-
+            for g in range(group):
+                obuf[j, d, g] = answer(j, d, g)
+                send_out(j, g, d).start()
+            return 0
+
+        lax.fori_loop(0, heads - 1, remote, 0)
+        own_q(j).wait()
         for g in range(group):
-            h = j * group + g
-            result = attend(
-                qbuf[j, d, :, g * HD:(g + 1) * HD],
-                [kv[j, 0, n * block:(n + 1) * block] for n in range(levels + 1)]
-                + [kv[j, 0, (levels + 1) * block:]],
-                [kv[j, 1, n * block:(n + 1) * block] for n in range(levels + 1)]
-                + [kv[j, 1, (levels + 1) * block:]],
-                [jnp.float32(0.0)] + [table[l, h] for l in range(levels + 1)],
-                scale,
-            )
-            obuf[j, d, g] = result.astype(bf16)
-
-            @pl.when(turn < heads - 1)
-            def _():
-                send_out(j, g, d).start()
-
-            @pl.when(turn == heads - 1)
-            def _():
-                own_out(j, g).start()
-
+            out_ref[:, out_cols(me, j, g)] = answer(j, 0, g)
         return 0
 
-    lax.fori_loop(0, kv_local * heads, one, 0)
+    lax.fori_loop(0, kv_local, one, 0)
 
     send_core().wait_send()
     for d in range(1, heads):
@@ -323,7 +320,6 @@
         for d in range(1, heads):
             send_q(j, d).wait_send()
         for g in range(group):
-            own_out(j, g).wait()
             for d in range(1, heads):
                 send_out(j, g, d).wait_send()
                 came_out(j, g, d).wait_recv()
@@ -336,18 +332,23 @@
     kv_local = keys.shape[1] // HD // heads
     group = level_bias.shape[0] // kv_local
     anchors = anchor_positions.shape[0]
-    smem = pl.BlockSpec(memory_space=pltpu.SMEM)
     vmem = pl.BlockSpec(memory_space=pltpu.VMEM)
     hbm = pl.BlockSpec(memory_space=pl.ANY)
     dma = pltpu.SemaphoreType.DMA
     anchor_shape = (kv_local, anchors, HD)
     bf16 = jnp.bfloat16
+    grant = (61 << 20) - 500_000 - queries.size * queries.dtype.itemsize
     return pl.pallas_call(
         functools.partial(kernel, heads, levels, kv_local, group),
-        in_specs=[smem, smem, smem, vmem, hbm, hbm, hbm],
-        out_specs=hbm,
-        out_shape=jax.ShapeDtypeStruct(queries.shape, queries.dtype),
+        in_specs=[hbm] * 7,
+        out_specs=vmem,
+        out_shape=pltpu.VMEM(queries.shape, queries.dtype),
         scratch_shapes=[
+            pltpu.SMEM(level_bias.shape[::-1], level_bias.dtype),
+            pltpu.SMEM(anchor_bias.shape, anchor_bias.dtype),
+            pltpu.SMEM(partners.shape, partners.dtype),
+            pltpu.VMEM((1, anchors), anchor_positions.dtype),
+            dma((4,)),
             pltpu.VMEM((kv_local, 2, (levels + 1) * heads * t + anchors, HD), bf16),
             pltpu.VMEM((kv_local, heads, t, group * HD), bf16),
             pltpu.VMEM((kv_local, heads, group, t, HD), bf16),
@@ -359,7 +360,7 @@
             pltpu.VMEM((levels,) + anchor_shape, bf16),
             pltpu.VMEM((levels,) + anchor_shape, bf16),
             pltpu.SMEM((levels + 1, kv_local * group), jnp.float32),
-            dma((kv_local, 2)), dma((2,)), dma((kv_local,)), dma((kv_local, group)),
+            dma((kv_local, 2)), dma((2,)), dma((kv_local,)),
             dma((kv_local, 2, heads)), dma((kv_local, 2, heads)),
             dma((kv_local, heads)), dma((kv_local, heads)),
             dma((kv_local, group, heads)), dma((kv_local, group, heads)),
@@ -367,7 +368,8 @@
             dma, dma, dma((heads,)), dma((heads,)), dma((levels,)), dma((levels,)),
             dma((kv_local,)), dma((kv_local,)), dma((kv_local,)),
         ],
-        compiler_params=pltpu.CompilerParams(collective_id=0, has_side_effects=True),
+        compiler_params=pltpu.CompilerParams(
+            vmem_limit_bytes=grant, collective_id=0, has_side_effects=True),
         name="attend",
     )(level_bias.T, anchor_bias, partners, anchor_positions[None, :], keys, values, queries)
 

time: 78.7 us -> 77 us (0.978)
  local copies, waits for them, and re-layouts: 3.13 us -> 1.32 us
    unnamed x1, local copies, waits for them, and re-layouts: 3.13 us -> 1.32 us
where the time goes in v2:
time: 77 us; the launch traced here: 76.5 us
  Pallas kernels  75.2 us (98%)
  local copies, waits for them, and re-layouts  1.32 us (2%)
    pallas_call x1, Pallas kernels, on_device(): pl.pallas_call(functools.partial(kernel, heads, levels, kv_local, group),...  75.2 us

profile of v2, /device:TPU:0, one launch (start us, length us, event | category | flops | bytes accessed | tf_op | source)
XLA Modules:
  0.0 76.5 jit_solution(16951810351610867777)
XLA Ops:
  0.0 75.2 %attend.1 = bf16[256,4096]{1,0:T(8,128)(2,1)S(1)} custom-call(f32[4,16]{1,0:T(4,128)} %bitcast.2, f32[16]{0:T(128)} %anchor_hbm.1, s32[1,4]{1,0:T(1,128)} %partners_hbm.1, s32[1,64]{1,0:T(1,128)} %bitcast.3, bf16[256,1024]{1,0:T(8,128)(2,1)} %keys_ref.1, bf16[256,1024]{1,0:T(8,128)(2,1)} %values_ref.1, bf16[256,4096]{1,0:T(8,128)(2,1)} %queries_ref.1), custom_call_target="tpu_custom_call" | custom-call | tf_op jit(solution)/shard_map/attend/pallas_call | solution.py:341
  75.2 1.3 %copy.9 = bf16[256,4096]{1,0:T(8,128)(2,1)} copy(bf16[256,4096]{1,0:T(8,128)(2,1)S(1)} %attend.1) | data formatting | bytes 4194304

commit v3 on v2

--- a/solution.py
+++ b/solution.py
@@ -293,6 +293,7 @@
             send_q(j, d).wait_recv()
             for g in range(group):
                 obuf[j, d, g] = answer(j, d, g)
+            for g in range(group):
                 send_out(j, g, d).start()
             return 0
 

time: 77 us -> 69.9 us (0.908)
  Pallas kernels: 75.2 us -> 68.4 us
    pallas_call x1, Pallas kernels: 75.2 us -> 68.4 us  [on_device(): pl.pallas_call(functools.partial(kernel, heads, levels, kv_local, group),...]
where the time goes in v3:
time: 69.9 us; the launch traced here: 69.8 us
  Pallas kernels  68.4 us (98%)
  local copies, waits for them, and re-layouts  1.32 us (2%)
    pallas_call x1, Pallas kernels, on_device(): pl.pallas_call(functools.partial(kernel, heads, levels, kv_local, group),...  68.4 us

profile of v3, /device:TPU:0, one launch (start us, length us, event | category | flops | bytes accessed | tf_op | source)
XLA Modules:
  0.0 69.8 jit_solution(9623262198946345570)
XLA Ops:
  0.0 68.4 %attend.1 = bf16[256,4096]{1,0:T(8,128)(2,1)S(1)} custom-call(f32[4,16]{1,0:T(4,128)} %bitcast.2, f32[16]{0:T(128)} %anchor_hbm.1, s32[1,4]{1,0:T(1,128)} %partners_hbm.1, s32[1,64]{1,0:T(1,128)} %bitcast.3, bf16[256,1024]{1,0:T(8,128)(2,1)} %keys_ref.1, bf16[256,1024]{1,0:T(8,128)(2,1)} %values_ref.1, bf16[256,4096]{1,0:T(8,128)(2,1)} %queries_ref.1), custom_call_target="tpu_custom_call" | custom-call | tf_op jit(solution)/shard_map/attend/pallas_call | solution.py:342
  68.4 1.3 %copy.9 = bf16[256,4096]{1,0:T(8,128)(2,1)} copy(bf16[256,4096]{1,0:T(8,128)(2,1)S(1)} %attend.1) | data formatting | bytes 4194304

commit v4 on v3

--- a/solution.py
+++ b/solution.py
@@ -38,11 +38,11 @@
     heads, levels, kv_local, group,
     level_hbm, anchor_hbm, partners_hbm, places_hbm, keys_ref, values_ref, queries_ref, out_ref,
     level_ref, anchor_ref, partners_ref, places_ref, small_sem,
-    kv, qbuf, obuf, full, part, part_in, head_out, head_in, carry, carry_in, table,
+    kv, qbuf, obuf, full, part, part_in, head_out, head_in, pair, pair_in, carry, carry_in, table,
     own_sem, full_sem, own_q_sem,
     x_send, x_recv, q_send, q_recv, o_send, o_recv, lv_send, lv_recv,
-    core_send, core_recv, head_send, head_recv, carry_send, carry_recv,
-    last_sem, last_send, last_recv,
+    core_send, core_recv, head_send, head_recv, pair_send, pair_recv, carry_send, carry_recv,
+    last_sem, half_send, half_recv, last_send, last_recv,
 ):
     me = lax.axis_index("head")
     seat = lax.axis_index("seq")
@@ -55,6 +55,8 @@
     bf16 = jnp.bfloat16
     sources = (keys_ref, values_ref)
     mine = lax.rem(seat, 2)
+    side = lax.rem(lax.div(seat, 2), 2)
+    half = anchors // 2
 
     def peer(d):
         return lax.rem(me + d, heads)
@@ -70,6 +72,9 @@
         return pl.ds(pl.multiple_of(n * block + r * t, t), t)
 
     anchor_rows = pl.ds((levels + 1) * block, anchors)
+
+    def half_rows(which):
+        return pl.ds(pl.multiple_of((levels + 1) * block + which * half, 16), half)
 
     def to_head(src, dst, send, recv, d):
         return pltpu.make_async_remote_copy(
@@ -124,23 +129,36 @@
         return to_level(part.at[1 - mine], part_in, core_send, core_recv, 0)
 
     def send_part(d):
-        return to_head(head_out.at[d], head_in.at[d], head_send.at[d], head_recv.at[d], d)
+        return to_head(head_out.at[peer(d)], head_in.at[d], head_send.at[d], head_recv.at[d], d)
+
+    def send_pair():
+        return to_level(pair.at[1 - side], pair_in, pair_send, pair_recv, 1)
 
     def send_carry(i, l):
         return to_level(carry.at[i], carry_in.at[i], carry_send.at[i], carry_recv.at[i], l)
 
-    def own_last(j):
+    def own_half(j):
         return pltpu.make_async_copy(
-            carry.at[levels - 1, j], kv.at[j, mine, anchor_rows], last_sem.at[j])
+            carry.at[levels - 2, j], kv.at[j, mine, half_rows(side)], last_sem.at[j])
+
+    def send_half(j):
+        return to_level(
+            carry.at[levels - 2, j], kv.at[j, mine, half_rows(side)],
+            half_send.at[j], half_recv.at[j], 1)
+
+    def half_came(j):
+        return to_level(
+            carry.at[levels - 2, j], kv.at[j, mine, half_rows(1 - side)],
+            half_send.at[j], half_recv.at[j], 1)
 
     def send_last(j):
         return to_level(
-            carry.at[levels - 1, j], kv.at[j, mine, anchor_rows],
+            kv.at[j, mine, anchor_rows], kv.at[j, mine, anchor_rows],
             last_send.at[j], last_recv.at[j], 0)
 
     def last_came(j):
         return to_level(
-            carry.at[levels - 1, j], kv.at[j, 1 - mine, anchor_rows],
+            kv.at[j, mine, anchor_rows], kv.at[j, 1 - mine, anchor_rows],
             last_send.at[j], last_recv.at[j], 0)
 
     def out_cols(owner, j, g):
@@ -199,11 +217,13 @@
     selector = jnp.where(places == token, 1.0, 0.0).astype(bf16)
     for c in range(2):
         full_copy(c).wait()
-        for d in range(heads):
+        found = lax.dot_general(
+            selector, full[c], (((0,), (0,)), ((), ())), preferred_element_type=jnp.float32)
+        found = found.astype(bf16)
+        for owner in range(heads):
             for j in range(kv_local):
-                part[c, d, j] = lax.dot_general(
-                    selector, full[c, :, cols(peer(d), j, HD)], (((0,), (0,)), ((), ())),
-                    preferred_element_type=jnp.float32).astype(bf16)
+                at = (owner * kv_local + j) * HD
+                part[c, owner, j] = found[:, at:at + HD]
     send_core().start()
     send_core().wait_recv()
     for d in range(heads):
@@ -239,34 +259,46 @@
     for c in range(2):
         own_copy(0, c).wait()
 
-    for i in range(3):
-        small(i).wait()
-
-    def fill(h, _):
-        for l in range(levels):
-            total = jnp.float32(0.0)
-            for m in range(levels):
-                total += jnp.where(partners_ref[0, m] == partner(l), level_ref[m, h], 0.0)
-            table[l, h] = total * LOG2E
-        table[levels, h] = anchor_ref[h] * LOG2E
-        return 0
-
-    lax.fori_loop(0, kv_local * group, fill, 0)
-
-    held = head_out[0].astype(jnp.float32)
+    def fill_table():
+        for i in range(3):
+            small(i).wait()
+        match = [[jnp.where(partners_ref[0, m] == partner(l), LOG2E, 0.0) for m in range(levels)]
+                 for l in range(levels)]
+
+        def fill(h, _):
+            biases = [level_ref[m, h] for m in range(levels)]
+            for l in range(levels):
+                table[l, h] = sum(match[l][m] * biases[m] for m in range(levels))
+            table[levels, h] = anchor_ref[h] * LOG2E
+            return 0
+
+        lax.fori_loop(0, kv_local * group, fill, 0)
+
+    held = head_out[me].astype(jnp.float32)
     for d in range(1, heads):
         send_part(d).wait_recv()
         held = held + head_in[d].astype(jnp.float32)
-    carry[0] = held.astype(bf16)
-    order = list(range(2, levels)) + ([1] if levels > 1 else [])
+    for which in range(2):
+        pair[which] = held[:, which * half:(which + 1) * half].astype(bf16)
+    send_pair().start()
+    push(1)
+    fill_table()
+    send_pair().wait_recv()
+    carry[0] = (pair[side].astype(jnp.float32) + pair_in[...].astype(jnp.float32)).astype(bf16)
+    order = list(range(2, levels))
     for i, l in enumerate(order):
         send_carry(i, l).start()
-        push(1)
+        push(2 if i else 1)
         send_carry(i, l).wait_recv()
         carry[i + 1] = (
             carry[i].astype(jnp.float32) + carry_in[i].astype(jnp.float32)).astype(bf16)
     for j in range(kv_local):
-        own_last(j).start()
+        own_half(j).start()
+        send_half(j).start()
+    push(2)
+    for j in range(kv_local):
+        own_half(j).wait()
+        half_came(j).wait_recv()
         send_last(j).start()
     push(len(pending))
 
@@ -281,7 +313,6 @@
         ).astype(bf16)
 
     def one(j, _):
-        own_last(j).wait()
         last_came(j).wait_recv()
         for l in range(levels):
             for c in range(2):
@@ -306,11 +337,13 @@
     lax.fori_loop(0, kv_local, one, 0)
 
     send_core().wait_send()
+    send_pair().wait_send()
     for d in range(1, heads):
         send_part(d).wait_send()
     for i, l in enumerate(order):
         send_carry(i, l).wait_send()
     for j in range(kv_local):
+        send_half(j).wait_send()
         send_last(j).wait_send()
         for c in range(2):
             for d in range(heads):
@@ -337,6 +370,7 @@
     hbm = pl.BlockSpec(memory_space=pl.ANY)
     dma = pltpu.SemaphoreType.DMA
     anchor_shape = (kv_local, anchors, HD)
+    half_shape = (kv_local, anchors // 2, HD)
     bf16 = jnp.bfloat16
     grant = (61 << 20) - 500_000 - queries.size * queries.dtype.itemsize
     return pl.pallas_call(
@@ -358,16 +392,18 @@
             pltpu.VMEM((heads,) + anchor_shape, bf16),
             pltpu.VMEM((heads,) + anchor_shape, bf16),
             pltpu.VMEM((heads,) + anchor_shape, bf16),
-            pltpu.VMEM((levels,) + anchor_shape, bf16),
-            pltpu.VMEM((levels,) + anchor_shape, bf16),
+            pltpu.VMEM((2,) + half_shape, bf16),
+            pltpu.VMEM(half_shape, bf16),
+            pltpu.VMEM((levels,) + half_shape, bf16),
+            pltpu.VMEM((levels,) + half_shape, bf16),
             pltpu.SMEM((levels + 1, kv_local * group), jnp.float32),
             dma((kv_local, 2)), dma((2,)), dma((kv_local,)),
             dma((kv_local, 2, heads)), dma((kv_local, 2, heads)),
             dma((kv_local, heads)), dma((kv_local, heads)),
             dma((kv_local, group, heads)), dma((kv_local, group, heads)),
             dma((kv_local, 2, heads, levels)), dma((kv_local, 2, heads, levels)),
-            dma, dma, dma((heads,)), dma((heads,)), dma((levels,)), dma((levels,)),
-            dma((kv_local,)), dma((kv_local,)), dma((kv_local,)),
+            dma, dma, dma((heads,)), dma((heads,)), dma, dma, dma((levels,)), dma((levels,)),
+            dma((kv_local,)), dma((kv_local,)), dma((kv_local,)), dma((kv_local,)), dma((kv_local,)),
         ],
         compiler_params=pltpu.CompilerParams(
             vmem_limit_bytes=grant, collective_id=0, has_side_effects=True),

time: 69.9 us -> 68.4 us (0.979)
  Pallas kernels: 68.4 us -> 66.9 us
    pallas_call x1, Pallas kernels: 68.4 us -> 66.9 us  [on_device(): pl.pallas_call(functools.partial(kernel, heads, levels, kv_local, group),...]
where the time goes in v4:
time: 68.4 us; the launch traced here: 68.2 us
  Pallas kernels  66.9 us (98%)
  local copies, waits for them, and re-layouts  1.32 us (2%)
    pallas_call x1, Pallas kernels, on_device(): pl.pallas_call(functools.partial(kernel, heads, levels, kv_local, group),...  66.9 us

profile of v4, /device:TPU:0, one launch (start us, length us, event | category | flops | bytes accessed | tf_op | source)
XLA Modules:
  0.0 68.2 jit_solution(4237014785946708005)
XLA Ops:
  0.0 66.9 %attend.1 = bf16[256,4096]{1,0:T(8,128)(2,1)S(1)} custom-call(f32[4,16]{1,0:T(4,128)} %bitcast.2, f32[16]{0:T(128)} %anchor_hbm.1, s32[1,4]{1,0:T(1,128)} %partners_hbm.1, s32[1,64]{1,0:T(1,128)} %bitcast.3, bf16[256,1024]{1,0:T(8,128)(2,1)} %keys_ref.1, bf16[256,1024]{1,0:T(8,128)(2,1)} %values_ref.1, bf16[256,4096]{1,0:T(8,128)(2,1)} %queries_ref.1), custom_call_target="tpu_custom_call" | custom-call | tf_op jit(solution)/shard_map/attend/pallas_call | solution.py:376
  66.9 1.3 %copy.9 = bf16[256,4096]{1,0:T(8,128)(2,1)} copy(bf16[256,4096]{1,0:T(8,128)(2,1)S(1)} %attend.1) | data formatting | bytes 4194304

commit v5 on v4

--- a/solution.py
+++ b/solution.py
@@ -288,7 +288,7 @@
     order = list(range(2, levels))
     for i, l in enumerate(order):
         send_carry(i, l).start()
-        push(2 if i else 1)
+        push(1)
         send_carry(i, l).wait_recv()
         carry[i + 1] = (
             carry[i].astype(jnp.float32) + carry_in[i].astype(jnp.float32)).astype(bf16)

time: 68.4 us -> 68.1 us (level)
  no operation moved by 1% of the time
where the time goes in v5:
time: 68.1 us; the launch traced here: 67.9 us
  Pallas kernels  66.6 us (98%)
  local copies, waits for them, and re-layouts  1.32 us (2%)
    pallas_call x1, Pallas kernels, on_device(): pl.pallas_call(functools.partial(kernel, heads, levels, kv_local, group),...  66.6 us

profile of v5, /device:TPU:0, one launch (start us, length us, event | category | flops | bytes accessed | tf_op | source)
XLA Modules:
  0.0 67.9 jit_solution(16734754786416653005)
XLA Ops:
  0.0 66.6 %attend.1 = bf16[256,4096]{1,0:T(8,128)(2,1)S(1)} custom-call(f32[4,16]{1,0:T(4,128)} %bitcast.2, f32[16]{0:T(128)} %anchor_hbm.1, s32[1,4]{1,0:T(1,128)} %partners_hbm.1, s32[1,64]{1,0:T(1,128)} %bitcast.3, bf16[256,1024]{1,0:T(8,128)(2,1)} %keys_ref.1, bf16[256,1024]{1,0:T(8,128)(2,1)} %values_ref.1, bf16[256,4096]{1,0:T(8,128)(2,1)} %queries_ref.1), custom_call_target="tpu_custom_call" | custom-call | tf_op jit(solution)/shard_map/attend/pallas_call | solution.py:376
  66.6 1.3 %copy.9 = bf16[256,4096]{1,0:T(8,128)(2,1)} copy(bf16[256,4096]{1,0:T(8,128)(2,1)S(1)} %attend.1) | data formatting | bytes 4194304

commit v6 on v5

--- a/solution.py
+++ b/solution.py
@@ -233,7 +233,10 @@
         send_part(d).start()
     for j in range(1, kv_local):
         push_kv(j)
-    for j in range(kv_local):
+        if j == kv_local - 2:
+            for d in range(1, heads):
+                send_q(0, d).start()
+    for j in range(0 if kv_local < 3 else 1, kv_local):
         for d in range(1, heads):
             send_q(j, d).start()
 

time: 68.1 us -> 68.1 us (level)
  no operation moved by 1% of the time
where the time goes in v6:
time: 68.1 us; the launch traced here: 67.9 us
  Pallas kernels  66.6 us (98%)
  local copies, waits for them, and re-layouts  1.32 us (2%)
    pallas_call x1, Pallas kernels, on_device(): pl.pallas_call(functools.partial(kernel, heads, levels, kv_local, group),...  66.6 us

profile of v6, /device:TPU:0, one launch (start us, length us, event | category | flops | bytes accessed | tf_op | source)
XLA Modules:
  0.0 67.9 jit_solution(10797156615388251780)
XLA Ops:
  0.0 66.6 %attend.1 = bf16[256,4096]{1,0:T(8,128)(2,1)S(1)} custom-call(f32[4,16]{1,0:T(4,128)} %bitcast.2, f32[16]{0:T(128)} %anchor_hbm.1, s32[1,4]{1,0:T(1,128)} %partners_hbm.1, s32[1,64]{1,0:T(1,128)} %bitcast.3, bf16[256,1024]{1,0:T(8,128)(2,1)} %keys_ref.1, bf16[256,1024]{1,0:T(8,128)(2,1)} %values_ref.1, bf16[256,4096]{1,0:T(8,128)(2,1)} %queries_ref.1), custom_call_target="tpu_custom_call" | custom-call | tf_op jit(solution)/shard_map/attend/pallas_call | solution.py:379
  66.6 1.3 %copy.9 = bf16[256,4096]{1,0:T(8,128)(2,1)} copy(bf16[256,4096]{1,0:T(8,128)(2,1)S(1)} %attend.1) | data formatting | bytes 4194304
